TPU v7x, 32 devices: a whole 2x2x4 slice. The times are simulated.
32 devices in a mesh: space: 4 (over x, core), mem: 8 (over z, y).
Axes of the slice: x: 2, y: 2, z: 4, core: 2. Of those that a mesh axis runs over, the one named last changes fastest.
Arguments:
- prior_ensemble: float32 [512, 8192], P('mem', 'space'), may hold values from -5 to 5
- terminal_particles: float32 [512, 8192], P(None, ('space', 'mem')), may hold values from -5 to 5
- reverse_perturbation: float32 [3, 512, 8192], P(None, None, ('space', 'mem')), may hold values from -6 to 6
- measured_angles: float32 [8192], P(('space', 'mem')), may hold values from -1.3 to 1.3
Outputs:
- analysis: float32 [512, 8192], P(None, ('space', 'mem'))
All inputs are finite; a program needn't handle non-finite values.
Results may differ from a plain program's by a relative error of at most 0.0003.
Values sent between devices are 32-bit elements; how exact they have to be, the bound alone decides.
A program may use at most 64 MiB of HBM per device.

v0:
```python
import functools
import math

import jax
import jax.numpy as jnp
from jax import lax
from jax.experimental import pallas as pl
from jax.experimental.pallas import tpu as pltpu
from jax.sharding import PartitionSpec as P

ITERS = 3
CHUNKS = 4
CORES = 2
SUBLANES = 8
LANES = 128
MESH = pl.DeviceIdType.MESH


def split(a, parts):
    out = []
    for _ in range(parts):
        out.append(a.astype(jnp.bfloat16))
        a = a - out[-1].astype(jnp.float32)
    return out


def product(a, parts, contract_b):
    n = a.shape[0]
    lhs = split(a, len(parts))
    total = None
    for i in reversed(range(len(parts))):
        rows = lhs[: len(parts) - i]
        both = lax.dot_general(
            jnp.concatenate(rows, axis=0),
            parts[i],
            (((1,), (contract_b,)), ((), ())),
            preferred_element_type=jnp.float32,
        )
        for j in reversed(range(len(rows))):
            term = both[j * n : (j + 1) * n]
            total = term if total is None else total + term
    return total


def arctan(x):
    a = jnp.abs(x)
    big = a > 2.414213562373095
    mid = a > 0.4142135623730950
    num = jnp.where(big, -1.0, jnp.where(mid, a - 1.0, a))
    den = jnp.where(big, a, jnp.where(mid, a + 1.0, 1.0))
    base = jnp.where(big, math.pi / 2, jnp.where(mid, math.pi / 4, 0.0))
    r = num / den
    s = r * r
    poly = ((8.05374449538e-2 * s - 1.38776856032e-1) * s + 1.99777106478e-1) * s
    poly = (poly - 3.33329491539e-1) * s * r + r
    y = base + poly
    return jnp.where(x < 0.0, -y, y)


def rows_at(start, size):
    return pl.ds(pl.multiple_of(start, SUBLANES), size)


def kernel(
    plan,
    prior,
    terminal,
    perturbation,
    angles,
    out,
    x,
    z,
    noise,
    seen,
    gram,
    xy_in,
    part,
    z_in,
    numer,
    w,
    xb,
    send,
    recv,
    once_send,
    once_recv,
    local,
):
    n_space, n_mem, ny, nz, scatter_z, mixed, temper = plan
    nxy = (n_space // CORES) * ny
    chunks, rows, _ = gram.shape
    rows3 = rows // nxy
    samples = z.shape[0]
    members = prior.shape[0]
    variables = terminal.shape[1]
    lanes = numer.shape[3]

    sp = lax.axis_index("space")
    me = lax.axis_index("mem")
    core = lax.rem(sp, CORES)
    other = 1 - core
    xi = lax.div(sp, CORES)
    yi = lax.rem(me, ny)
    zi = lax.div(me, ny)

    core_dev = (xi * CORES + other, me)

    here = {"x": xi, "y": yi, "z": zi, "one": 0}
    size = {"x": n_space // CORES, "y": ny, "z": nz, "one": 1}

    def position(axes):
        return here[axes[0]] * size[axes[1]] + here[axes[1]]

    def peer(axes, d):
        p = lax.rem(position(axes) + d, size[axes[0]] * size[axes[1]])
        at = dict(here)
        at[axes[0]] = lax.div(p, size[axes[1]])
        at[axes[1]] = lax.rem(p, size[axes[1]])
        return p, (at["x"] * CORES + core, at["z"] * ny + at["y"])

    orders = [(("x", "y"), ("one", "z"))]
    if mixed:
        orders += [orders[0][::-1], orders[0], orders[0]]
    orders = [orders[c % len(orders)] for c in range(chunks)]

    def mem_peer(d):
        p = lax.rem(me + d, n_mem)
        return p, (sp, p)

    def cols(p):
        return pl.ds(pl.multiple_of(p * variables, variables), variables)

    mine = cols(core)
    my_samples = rows_at(core * samples, samples)
    its_samples = rows_at(other * samples, samples)
    my_members = rows_at(me * members, members)

    loads = [
        pltpu.make_async_copy(
            prior.at[:, cols(me)], x.at[my_members, mine], local.at[0]
        ),
        pltpu.make_async_copy(terminal.at[my_samples, :], z.at[:, mine], local.at[1]),
        pltpu.make_async_copy(angles, seen.at[:, mine], local.at[2]),
        pltpu.make_async_copy(
            perturbation.at[:, my_samples, :], noise.at[:, :, mine], local.at[3]
        ),
    ]
    for copy in loads:
        copy.start()

    barrier = pltpu.get_barrier_semaphore()
    greet = [core_dev]
    for axes in sorted({axes for order in orders for axes in order}):
        n = size[axes[0]] * size[axes[1]]
        greet += [peer(axes, d)[1] for d in range(1, n)]
    greet += [mem_peer(d)[1] for d in range(1, n_mem)]
    for dev in greet:
        pl.semaphore_signal(barrier, inc=1, device_id=dev, device_id_type=MESH)
    pl.semaphore_wait(barrier, len(greet))

    def put_once(src, dst, i, dev):
        copy = pltpu.make_async_remote_copy(
            src_ref=src,
            dst_ref=dst,
            send_sem=once_send.at[i],
            recv_sem=once_recv.at[i],
            device_id=dev,
            device_id_type=MESH,
        )
        copy.start()
        return copy

    exchange = []
    for d in range(1, n_mem):
        p, dev = mem_peer(d)
        exchange.append(put_once(prior.at[:, cols(p)], x.at[my_members, mine], d - 1, dev))
    i = n_mem - 1
    swaps = [
        put_once(terminal.at[its_samples, :], z.at[:, mine], i, core_dev),
        put_once(angles, seen.at[:, mine], i + 1, core_dev),
        put_once(prior.at[:, cols(me)], x.at[my_members, mine], i + 2, core_dev),
        put_once(perturbation.at[:, its_samples, :], noise.at[:, :, mine], i + 3, core_dev),
    ]
    i = i + 4
    for d, copy in enumerate(exchange):
        copy.wait_recv()
        theirs = rows_at(lax.rem(me + n_mem - d - 1, n_mem) * members, members)
        swaps.append(put_once(x.at[theirs, mine], x.at[theirs, mine], i + d, core_dev))
    i = i + n_mem - 1
    for copy in loads:
        copy.wait()
    for copy in swaps:
        copy.wait_recv()

    xs = x[...]
    for j, piece in enumerate(split(xs, 3)):
        xb[j] = piece
    norms = jnp.zeros((SUBLANES, xs.shape[0]), jnp.float32)
    for piece in reversed(split(xs * xs, 3)):
        norms = norms + lax.dot_general(
            jnp.ones((SUBLANES, xs.shape[1]), jnp.bfloat16),
            piece,
            (((1,), (1,)), ((), ())),
            preferred_element_type=jnp.float32,
        )
    norms = norms[:1]

    first_z = nxy - 1
    first_gz = first_z + nz - 1
    first_gxy = first_gz + nz - 1

    def chunk(c):
        where = pl.ds(c * rows, rows)
        first, second = orders[c]
        mine_xy = rows_at(position(first) * rows3, rows3)
        z_at = position(second)
        for k in range(ITERS):
            t = 1.0 - k / ITERS
            dt = 1.0 / ITERS
            alpha = 1.0 - 0.5 * t
            drift = -0.5 / alpha
            g2 = 1.0 + t / alpha
            damp = 1.0 - t
            started = []

            def put(src, dst, i, dev):
                copy = pltpu.make_async_remote_copy(
                    src_ref=src,
                    dst_ref=dst,
                    send_sem=send.at[k % 2, c, i],
                    recv_sem=recv.at[k % 2, c, i],
                    device_id=dev,
                    device_id_type=MESH,
                )
                copy.start()
                started.append(copy)
                return copy

            gram[c] = 2.0 * alpha * product(z[where, :], [xb[0], xb[1], xb[2]], 1) - alpha * alpha * norms
            group = []
            for d in range(1, nxy):
                p, dev = peer(first, d)
                group.append(
                    put(gram.at[c, rows_at(p * rows3, rows3), :], xy_in.at[c, d - 1], d - 1, dev)
                )
            yield
            total = gram[c, mine_xy, :]
            for d, copy in enumerate(group):
                copy.wait_recv()
                total = total + xy_in[c, d]
            group = []
            if scatter_z:
                for p in range(nz):
                    part[c, p] = total[:, p * lanes : (p + 1) * lanes]
            else:
                part[c, 0] = total
            for d in range(1, nz):
                p, dev = peer(second, d)
                src = part.at[c, p] if scatter_z else part.at[c, 0]
                group.append(put(src, z_in.at[k % 2, c, d - 1], first_z + d - 1, dev))
            yield
            block = part[c, z_at] if scatter_z else part[c, 0]
            for d, copy in enumerate(group):
                copy.wait_recv()
                block = block + z_in[k % 2, c, d]
            if scatter_z:
                numer[c, z_at] = block
                group = [
                    put(numer.at[c, z_at], numer.at[c, z_at], first_gz + d - 1, peer(second, d)[1])
                    for d in range(1, nz)
                ]
                yield
                for copy in group:
                    copy.wait_recv()
                block = jnp.concatenate([numer[c, p] for p in range(nz)], axis=1)
            logits = block / (2.0 * t * temper)
            e = jnp.exp(logits - jnp.max(logits, axis=1, keepdims=True))
            w[c, mine_xy, :] = e / jnp.sum(e, axis=1, keepdims=True)
            group = [
                put(w.at[c, mine_xy, :], w.at[c, mine_xy, :], first_gxy + d - 1, peer(first, d)[1])
                for d in range(1, nxy)
            ]
            yield
            for copy in group:
                copy.wait_recv()
            blend = product(w[c], [xb[0], xb[1]], 0)
            zs = z[where, :]
            score = -(zs - alpha * blend) / t + damp * 4.0 * (seen[...] - arctan(zs)) / (
                1.0 + zs * zs
            )
            z[where, :] = (
                zs + dt * (-drift * zs + g2 * score) + math.sqrt(dt * g2) * noise[k, where, :]
            )
            for copy in started:
                copy.wait_send()
        target = out.at[rows_at(core * samples + c * rows, rows), :]
        result = pltpu.make_async_copy(z.at[where, mine], target, local.at[4 + c])
        result.start()
        swap = put_once(z.at[where, cols(other)], target, i + c, core_dev)
        yield
        result.wait()
        swap.wait()

    running = [chunk(c) for c in range(chunks)]
    while running:
        still = []
        for item in running:
            try:
                next(item)
                still.append(item)
            except StopIteration:
                pass
        running = still
    for copy in exchange + swaps:
        copy.wait_send()


def per_device(prior, terminal, perturbation, angles):
    n_space, n_mem = lax.axis_size("space"), lax.axis_size("mem")
    samples, variables = terminal.shape
    members = prior.shape[0] * n_mem
    nx = n_space // CORES
    ny = math.gcd(nx, n_mem)
    nz = n_mem // ny
    nxy = nx * ny
    half = samples // CORES
    chunks = CHUNKS
    while chunks > 1 and half % (chunks * nxy * SUBLANES):
        chunks //= 2
    rows = half // chunks
    rows3 = rows // nxy
    scatter_z = members % (nz * LANES) == 0
    pieces = nz if scatter_z else 1
    lanes = members // pieces
    mixed = nxy == nz and scatter_z
    temper = math.sqrt(variables * n_space * n_mem)
    f32 = jnp.float32
    exchanges = 2 * (nxy - 1 + nz - 1)
    once = 2 * (n_mem - 1) + 4 + chunks
    iters = perturbation.shape[0]
    anywhere = pl.BlockSpec(memory_space=pl.ANY)
    return pl.pallas_call(
        functools.partial(kernel, (n_space, n_mem, ny, nz, scatter_z, mixed, temper)),
        out_shape=jax.ShapeDtypeStruct((samples, variables), f32),
        in_specs=[anywhere] * 4,
        out_specs=anywhere,
        scratch_shapes=[
            pltpu.VMEM((members, CORES * variables), f32),
            pltpu.VMEM((half, CORES * variables), f32),
            pltpu.VMEM((iters, half, CORES * variables), f32),
            pltpu.VMEM((1, CORES * variables), f32),
            pltpu.VMEM((chunks, rows, members), f32),
            pltpu.VMEM((chunks, nxy - 1, rows3, members), f32),
            pltpu.VMEM((chunks, pieces, rows3, lanes), f32),
            pltpu.VMEM((2, chunks, nz - 1, rows3, lanes), f32),
            pltpu.VMEM((chunks, pieces, rows3, lanes), f32),
            pltpu.VMEM((chunks, rows, members), f32),
            pltpu.VMEM((3, members, CORES * variables), jnp.bfloat16),
            pltpu.SemaphoreType.DMA((2, chunks, exchanges)),
            pltpu.SemaphoreType.DMA((2, chunks, exchanges)),
            pltpu.SemaphoreType.DMA((once,)),
            pltpu.SemaphoreType.DMA((once,)),
            pltpu.SemaphoreType.DMA((4 + chunks,)),
        ],
        compiler_params=pltpu.CompilerParams(collective_id=0, has_side_effects=True),
    )(prior, terminal, perturbation, angles.reshape(1, variables))


def solution(mesh):
    in_specs = (
        P("mem", "space"),
        P(None, ("space", "mem")),
        P(None, None, ("space", "mem")),
        P(("space", "mem")),
    )
    out_specs = P(None, ("space", "mem"))
    return jax.shard_map(
        per_device, mesh=mesh, in_specs=in_specs, out_specs=out_specs, check_vma=False
    )
```

profile of v0, /device:TPU:0, one launch (start us, length us, event | category | flops | bytes accessed | tf_op | source)
XLA Modules:
  0.0 77.1 jit_solution(13203608879034148212)
XLA Ops:
  0.0 75.3 %shard_map.46 = f32[512,256]{1,0:T(8,128)} custom-call(f32[64,2048]{1,0:T(8,128)} %prior.1, f32[512,256]{1,0:T(8,128)} %terminal.1, f32[3,512,256]{2,1,0:T(8,128)} %perturbation.1, f32[1,256]{1,0:T(1,128)} %bitcast.1), custom_call_target="tpu_custom_call" | custom-call | tf_op jit(solution)/shard_map/pallas_call | solution.py:341
  75.3 1.9 %copy.6 = f32[512,256]{1,0:T(8,128)} copy(f32[512,256]{1,0:T(8,128)} %shard_map.46) | data formatting | bytes 1048576
where the time goes:
time: 77.3 us; the launch traced here: 77.1 us
  Pallas kernels  75.3 us (97%)
  local copies, waits for them, and re-layouts  1.87 us (2%)
    pallas_call x1, Pallas kernels, per_device(): pl.pallas_call(functools.partial(kernel, (n_space, n_mem, ny, nz, scatter...  75.3 us
    unnamed x1, local copies, waits for them, and re-layouts  1.87 us

commit v1 on v0

--- a/solution.py
+++ b/solution.py
@@ -12,6 +12,8 @@
 CHUNKS = 4
 CORES = 2
 SUBLANES = 8
+SQUARE = 3
+SETS = 4
 LANES = 128
 MESH = pl.DeviceIdType.MESH
 
@@ -59,6 +61,12 @@
 
 def rows_at(start, size):
     return pl.ds(pl.multiple_of(start, SUBLANES), size)
+
+
+def constants(k):
+    t = 1.0 - k / ITERS
+    alpha = 1.0 - 0.5 * t
+    return t, alpha, -0.5 / alpha, 1.0 + t / alpha, 1.0 - t
 
 
 def kernel(
@@ -78,21 +86,27 @@
     z_in,
     numer,
     w,
+    square,
     xb,
+    kb,
+    pull,
     send,
     recv,
+    give_send,
+    give_recv,
     once_send,
     once_recv,
     local,
 ):
     n_space, n_mem, ny, nz, scatter_z, mixed, temper = plan
     nxy = (n_space // CORES) * ny
-    chunks, rows, _ = gram.shape
+    _, chunks, rows, _ = gram.shape
     rows3 = rows // nxy
     samples = z.shape[0]
     members = prior.shape[0]
     variables = terminal.shape[1]
-    lanes = numer.shape[3]
+    lanes = numer.shape[4]
+    dt = 1.0 / ITERS
 
     sp = lax.axis_index("space")
     me = lax.axis_index("mem")
@@ -186,9 +200,9 @@
         theirs = rows_at(lax.rem(me + n_mem - d - 1, n_mem) * members, members)
         swaps.append(put_once(x.at[theirs, mine], x.at[theirs, mine], i + d, core_dev))
     i = i + n_mem - 1
-    for copy in loads:
+    for copy in loads[:3]:
         copy.wait()
-    for copy in swaps:
+    for copy in swaps[:3] + swaps[4:]:
         copy.wait_recv()
 
     xs = x[...]
@@ -204,113 +218,205 @@
         )
     norms = norms[:1]
 
+    all_sent = []
+    inbound = {}
     first_z = nxy - 1
     first_gz = first_z + nz - 1
-    first_gxy = first_gz + nz - 1
-
-    def chunk(c):
-        where = pl.ds(c * rows, rows)
-        first, second = orders[c]
-        mine_xy = rows_at(position(first) * rows3, rows3)
-        z_at = position(second)
-        for k in range(ITERS):
-            t = 1.0 - k / ITERS
-            dt = 1.0 / ITERS
-            alpha = 1.0 - 0.5 * t
-            drift = -0.5 / alpha
-            g2 = 1.0 + t / alpha
-            damp = 1.0 - t
-            started = []
-
-            def put(src, dst, i, dev):
-                copy = pltpu.make_async_remote_copy(
-                    src_ref=src,
-                    dst_ref=dst,
-                    send_sem=send.at[k % 2, c, i],
-                    recv_sem=recv.at[k % 2, c, i],
-                    device_id=dev,
-                    device_id_type=MESH,
-                )
-                copy.start()
-                started.append(copy)
-                return copy
-
-            gram[c] = 2.0 * alpha * product(z[where, :], [xb[0], xb[1], xb[2]], 1) - alpha * alpha * norms
-            group = []
-            for d in range(1, nxy):
-                p, dev = peer(first, d)
-                group.append(
-                    put(gram.at[c, rows_at(p * rows3, rows3), :], xy_in.at[c, d - 1], d - 1, dev)
-                )
-            yield
-            total = gram[c, mine_xy, :]
-            for d, copy in enumerate(group):
-                copy.wait_recv()
-                total = total + xy_in[c, d]
-            group = []
-            if scatter_z:
-                for p in range(nz):
-                    part[c, p] = total[:, p * lanes : (p + 1) * lanes]
-            else:
-                part[c, 0] = total
-            for d in range(1, nz):
-                p, dev = peer(second, d)
-                src = part.at[c, p] if scatter_z else part.at[c, 0]
-                group.append(put(src, z_in.at[k % 2, c, d - 1], first_z + d - 1, dev))
-            yield
-            block = part[c, z_at] if scatter_z else part[c, 0]
-            for d, copy in enumerate(group):
-                copy.wait_recv()
-                block = block + z_in[k % 2, c, d]
-            if scatter_z:
-                numer[c, z_at] = block
-                group = [
-                    put(numer.at[c, z_at], numer.at[c, z_at], first_gz + d - 1, peer(second, d)[1])
-                    for d in range(1, nz)
-                ]
-                yield
-                for copy in group:
-                    copy.wait_recv()
-                block = jnp.concatenate([numer[c, p] for p in range(nz)], axis=1)
-            logits = block / (2.0 * t * temper)
-            e = jnp.exp(logits - jnp.max(logits, axis=1, keepdims=True))
-            w[c, mine_xy, :] = e / jnp.sum(e, axis=1, keepdims=True)
-            group = [
-                put(w.at[c, mine_xy, :], w.at[c, mine_xy, :], first_gxy + d - 1, peer(first, d)[1])
-                for d in range(1, nxy)
+
+    def chunk_rows(c):
+        return pl.ds(c * rows, rows)
+
+    def owned(c):
+        return rows_at(position(orders[c][0]) * rows3, rows3)
+
+    def remote(src, dst, sent, got, dev):
+        copy = pltpu.make_async_remote_copy(
+            src_ref=src,
+            dst_ref=dst,
+            send_sem=sent,
+            recv_sem=got,
+            device_id=dev,
+            device_id_type=MESH,
+        )
+        copy.start()
+        all_sent.append(copy)
+        return copy
+
+    def put(s, c, i, src, dst, dev):
+        return remote(src, dst, send.at[s, c, i], recv.at[s, c, i], dev)
+
+    def scatter(s, c, value):
+        gram[s, c] = value
+        first = orders[c][0]
+        group = []
+        for d in range(1, nxy):
+            p, dev = peer(first, d)
+            src = gram.at[s, c, rows_at(p * rows3, rows3), :]
+            group.append(put(s, c, d - 1, src, xy_in.at[s, c, d - 1], dev))
+        inbound[s, c] = group
+
+    def scatter_gram(k, c):
+        alpha = constants(k)[1]
+        inner = product(z[chunk_rows(c), :], [xb[0], xb[1], xb[2]], 1)
+        scatter(k, c, 2.0 * alpha * inner - alpha * alpha * norms)
+
+    def scatter_square(c):
+        at = rows_at(core * samples + c * rows, rows)
+        scatter(SQUARE, c, product(x[at, :], [xb[0], xb[1], xb[2]], 1))
+
+    def second(s, c):
+        after = orders[c][1]
+        total = gram[s, c, owned(c), :]
+        for d, copy in enumerate(inbound[s, c]):
+            copy.wait_recv()
+            total = total + xy_in[s, c, d]
+        if scatter_z:
+            for p in range(nz):
+                part[s, c, p] = total[:, p * lanes : (p + 1) * lanes]
+        else:
+            part[s, c, 0] = total
+        group = []
+        for d in range(1, nz):
+            p, dev = peer(after, d)
+            src = part.at[s, c, p] if scatter_z else part.at[s, c, 0]
+            group.append(put(s, c, first_z + d - 1, src, z_in.at[s, c, d - 1], dev))
+        inbound[s, c] = group
+
+    def third(s, c):
+        after = orders[c][1]
+        z_at = position(after) if scatter_z else 0
+        block = part[s, c, z_at]
+        for d, copy in enumerate(inbound[s, c]):
+            copy.wait_recv()
+            block = block + z_in[s, c, d]
+        numer[s, c, z_at] = block
+        inbound[s, c] = []
+        if scatter_z:
+            at = numer.at[s, c, z_at]
+            inbound[s, c] = [
+                put(s, c, first_gz + d - 1, at, at, peer(after, d)[1]) for d in range(1, nz)
             ]
-            yield
-            for copy in group:
-                copy.wait_recv()
-            blend = product(w[c], [xb[0], xb[1]], 0)
-            zs = z[where, :]
-            score = -(zs - alpha * blend) / t + damp * 4.0 * (seen[...] - arctan(zs)) / (
-                1.0 + zs * zs
-            )
-            z[where, :] = (
-                zs + dt * (-drift * zs + g2 * score) + math.sqrt(dt * g2) * noise[k, where, :]
-            )
-            for copy in started:
-                copy.wait_send()
+
+    def full(s, c):
+        for copy in inbound[s, c]:
+            copy.wait_recv()
+        if scatter_z:
+            return jnp.concatenate([numer[s, c, p] for p in range(nz)], axis=1)
+        return numer[s, c, 0]
+
+    def share(s, c, at):
+        first = orders[c][0]
+        inbound["share", s, c] = [
+            remote(at, at, give_send.at[s, c, d - 1], give_recv.at[s, c, d - 1], peer(first, d)[1])
+            for d in range(1, nxy)
+        ]
+
+    def arrived(s, c):
+        for copy in inbound["share", s, c]:
+            copy.wait_recv()
+
+    def share_weights(k, c, block):
+        logits = block / (2.0 * constants(k)[0] * temper)
+        e = jnp.exp(logits - jnp.max(logits, axis=1, keepdims=True))
+        w[k, c, owned(c), :] = e / jnp.sum(e, axis=1, keepdims=True)
+        share(k, c, w.at[k, c, owned(c), :])
+
+    def share_square(c):
+        at = rows_at(core * samples + c * rows + position(orders[c][0]) * rows3, rows3)
+        square[at, :] = full(SQUARE, c)
+        share(SQUARE, c, square.at[at, :])
+
+    def advance(k, c):
+        t, alpha, drift, g2, damp = constants(k)
+        where = chunk_rows(c)
+        zs = z[where, :]
+        seen_term = damp * 4.0 * (seen[...] - arctan(zs)) / (1.0 + zs * zs)
+        z[where, :] = (
+            zs
+            + dt * (-drift * zs + g2 * (seen_term - zs / t))
+            + math.sqrt(dt * g2) * noise[k, where, :]
+        )
+
+    def add_blend(k, c):
+        t, alpha, _, g2, _ = constants(k)
+        where = chunk_rows(c)
+        arrived(k, c)
+        blend = product(w[k, c], [xb[0], xb[1]], 0)
+        z[where, :] = z[where, :] + (dt * g2 * alpha / t) * blend
+
+    def pull_on(k):
+        t, alpha, _, g2, _ = constants(k)
+        scale = 2.0 * constants(k + 1)[1] * (dt * g2 * alpha / t)
+        mine_w = jnp.concatenate([w[k, c, owned(c), :] for c in range(chunks)], axis=0)
+        pull[k] = scale * product(mine_w, [kb[0], kb[1], kb[2]], 0)
+
+    each = range(chunks)
+    for c in each:
+        scatter_gram(0, c)
+    for c in each:
+        scatter_square(c)
+    loads[3].wait()
+    swaps[3].wait_recv()
+    for c in each:
+        advance(0, c)
+        scatter_gram(1, c)
+    for c in each:
+        second(0, c)
+    for c in each:
+        second(SQUARE, c)
+    for c in each:
+        third(0, c)
+    for c in each:
+        second(1, c)
+    for c in each:
+        share_weights(0, c, full(0, c))
+    for c in each:
+        third(SQUARE, c)
+    for c in each:
+        third(1, c)
+    for c in each:
+        share_square(c)
+    for c in each:
+        add_blend(0, c)
+        advance(1, c)
+        scatter_gram(2, c)
+    halves = []
+    for c in each:
+        arrived(SQUARE, c)
+        at = square.at[rows_at(core * samples + c * rows, rows), :]
+        halves.append(put_once(at, at, i + c, core_dev))
+    i = i + chunks
+    for c in each:
+        second(2, c)
+    for copy in halves:
+        copy.wait_recv()
+    for j, piece in enumerate(split(square[...], 3)):
+        kb[j] = piece
+    pull_on(0)
+    for c in each:
+        share_weights(1, c, full(1, c) + pull[0, pl.ds(c * rows3, rows3), :])
+    pull_on(1)
+    for c in each:
+        third(2, c)
+    for c in each:
+        add_blend(1, c)
+        advance(2, c)
+    for c in each:
+        share_weights(2, c, full(2, c) + pull[1, pl.ds(c * rows3, rows3), :])
+    results = []
+    for c in each:
+        add_blend(2, c)
+        where = chunk_rows(c)
         target = out.at[rows_at(core * samples + c * rows, rows), :]
         result = pltpu.make_async_copy(z.at[where, mine], target, local.at[4 + c])
         result.start()
-        swap = put_once(z.at[where, cols(other)], target, i + c, core_dev)
-        yield
-        result.wait()
-        swap.wait()
-
-    running = [chunk(c) for c in range(chunks)]
-    while running:
-        still = []
-        for item in running:
-            try:
-                next(item)
-                still.append(item)
-            except StopIteration:
-                pass
-        running = still
-    for copy in exchange + swaps:
+        results.append(result)
+        swaps.append(put_once(z.at[where, cols(other)], target, i + c, core_dev))
+    for copy in results:
+        copy.wait()
+    for copy in swaps[-chunks:]:
+        copy.wait_recv()
+    for copy in exchange + swaps + halves + all_sent:
         copy.wait_send()
 
 
@@ -318,6 +424,7 @@
     n_space, n_mem = lax.axis_size("space"), lax.axis_size("mem")
     samples, variables = terminal.shape
     members = prior.shape[0] * n_mem
+    assert members == samples
     nx = n_space // CORES
     ny = math.gcd(nx, n_mem)
     nz = n_mem // ny
@@ -334,8 +441,8 @@
     mixed = nxy == nz and scatter_z
     temper = math.sqrt(variables * n_space * n_mem)
     f32 = jnp.float32
-    exchanges = 2 * (nxy - 1 + nz - 1)
-    once = 2 * (n_mem - 1) + 4 + chunks
+    exchanges = nxy - 1 + 2 * (nz - 1)
+    once = 2 * (n_mem - 1) + 4 + 2 * chunks
     iters = perturbation.shape[0]
     anywhere = pl.BlockSpec(memory_space=pl.ANY)
     return pl.pallas_call(
@@ -348,15 +455,20 @@
             pltpu.VMEM((half, CORES * variables), f32),
             pltpu.VMEM((iters, half, CORES * variables), f32),
             pltpu.VMEM((1, CORES * variables), f32),
-            pltpu.VMEM((chunks, rows, members), f32),
-            pltpu.VMEM((chunks, nxy - 1, rows3, members), f32),
-            pltpu.VMEM((chunks, pieces, rows3, lanes), f32),
-            pltpu.VMEM((2, chunks, nz - 1, rows3, lanes), f32),
-            pltpu.VMEM((chunks, pieces, rows3, lanes), f32),
-            pltpu.VMEM((chunks, rows, members), f32),
+            pltpu.VMEM((SETS, chunks, rows, members), f32),
+            pltpu.VMEM((SETS, chunks, nxy - 1, rows3, members), f32),
+            pltpu.VMEM((SETS, chunks, pieces, rows3, lanes), f32),
+            pltpu.VMEM((SETS, chunks, nz - 1, rows3, lanes), f32),
+            pltpu.VMEM((SETS, chunks, pieces, rows3, lanes), f32),
+            pltpu.VMEM((iters, chunks, rows, members), f32),
+            pltpu.VMEM((members, members), f32),
             pltpu.VMEM((3, members, CORES * variables), jnp.bfloat16),
-            pltpu.SemaphoreType.DMA((2, chunks, exchanges)),
-            pltpu.SemaphoreType.DMA((2, chunks, exchanges)),
+            pltpu.VMEM((3, members, members), jnp.bfloat16),
+            pltpu.VMEM((iters - 1, chunks * rows3, members), f32),
+            pltpu.SemaphoreType.DMA((SETS, chunks, exchanges)),
+            pltpu.SemaphoreType.DMA((SETS, chunks, exchanges)),
+            pltpu.SemaphoreType.DMA((SETS, chunks, nxy - 1)),
+            pltpu.SemaphoreType.DMA((SETS, chunks, nxy - 1)),
             pltpu.SemaphoreType.DMA((once,)),
             pltpu.SemaphoreType.DMA((once,)),
             pltpu.SemaphoreType.DMA((4 + chunks,)),

time: 77.3 us -> 77 us (level)
  no operation moved by 1% of the time
where the time goes in v1:
time: 77 us; the launch traced here: 76.8 us
  Pallas kernels  75 us (97%)
  local copies, waits for them, and re-layouts  1.87 us (2%)
    pallas_call x1, Pallas kernels, per_device(): pl.pallas_call(functools.partial(kernel, (n_space, n_mem, ny, nz, scatter...  75 us
    unnamed x1, local copies, waits for them, and re-layouts  1.87 us

profile of v1, /device:TPU:0, one launch (start us, length us, event | category | flops | bytes accessed | tf_op | source)
XLA Modules:
  0.0 76.8 jit_solution(16652771233936157328)
XLA Ops:
  0.0 75.0 %shard_map.46 = f32[512,256]{1,0:T(8,128)} custom-call(f32[64,2048]{1,0:T(8,128)} %prior.1, f32[512,256]{1,0:T(8,128)} %terminal.1, f32[3,512,256]{2,1,0:T(8,128)} %perturbation.1, f32[1,256]{1,0:T(1,128)} %bitcast.1), custom_call_target="tpu_custom_call" | custom-call | tf_op jit(solution)/shard_map/pallas_call | solution.py:448
  75.0 1.9 %copy.6 = f32[512,256]{1,0:T(8,128)} copy(f32[512,256]{1,0:T(8,128)} %shard_map.46) | data formatting | bytes 1048576

commit v2 on v0

v2 whole, which is shorter than its diff:
```python
import functools
import math

import jax
import jax.numpy as jnp
from jax import lax
from jax.experimental import pallas as pl
from jax.experimental.pallas import tpu as pltpu
from jax.sharding import PartitionSpec as P

ITERS = 3
CHUNKS = 2
PARTS = 2
VMEM_LIMIT = 48 << 20
CORES = 2
SUBLANES = 8
LANES = 128
MESH = pl.DeviceIdType.MESH


def split(a, parts):
    out = []
    for _ in range(parts):
        out.append(a.astype(jnp.bfloat16))
        a = a - out[-1].astype(jnp.float32)
    return out


def product(a, parts, contract_b):
    n = a.shape[0]
    lhs = split(a, len(parts))
    total = None
    for i in reversed(range(len(parts))):
        rows = lhs[: len(parts) - i]
        both = lax.dot_general(
            jnp.concatenate(rows, axis=0),
            parts[i],
            (((1,), (contract_b,)), ((), ())),
            preferred_element_type=jnp.float32,
        )
        for j in reversed(range(len(rows))):
            term = both[j * n : (j + 1) * n]
            total = term if total is None else total + term
    return total


def arctan(x):
    a = jnp.abs(x)
    big = a > 2.414213562373095
    mid = a > 0.4142135623730950
    num = jnp.where(big, -1.0, jnp.where(mid, a - 1.0, a))
    den = jnp.where(big, a, jnp.where(mid, a + 1.0, 1.0))
    base = jnp.where(big, math.pi / 2, jnp.where(mid, math.pi / 4, 0.0))
    r = num / den
    s = r * r
    poly = ((8.05374449538e-2 * s - 1.38776856032e-1) * s + 1.99777106478e-1) * s
    poly = (poly - 3.33329491539e-1) * s * r + r
    y = base + poly
    return jnp.where(x < 0.0, -y, y)


def rows_at(start, size):
    return pl.ds(pl.multiple_of(start, SUBLANES), size)


def constants(k):
    t = 1.0 - k / ITERS
    alpha = 1.0 - 0.5 * t
    return t, alpha, -0.5 / alpha, 1.0 + t / alpha, 1.0 - t


def kernel(
    plan,
    prior,
    terminal,
    perturbation,
    angles,
    out,
    x,
    z,
    noise,
    seen,
    gram,
    sums,
    w,
    xb,
    sum_send,
    sum_recv,
    give_send,
    give_recv,
    once_send,
    once_recv,
    local,
):
    n_space, n_mem, scatter, temper = plan
    _, chunks, rows, members = gram.shape
    own_rows = rows // n_mem if scatter else rows
    samples = z.shape[0]
    block = prior.shape[0]
    variables = terminal.shape[1]
    nx = n_space // CORES
    dt = 1.0 / ITERS

    sp = lax.axis_index("space")
    me = lax.axis_index("mem")
    core = lax.rem(sp, CORES)
    xi = lax.div(sp, CORES)
    partner = (xi * CORES + 1 - core, me)

    def space_at(d):
        return lax.rem(sp + d + n_space, n_space)

    def x_at(d):
        return lax.rem(xi + d + nx, nx) * CORES + core

    def mem_to(d):
        if n_mem & (n_mem - 1):
            return lax.rem(me + d, n_mem)
        return flipped(d)

    def mem_from(d):
        if n_mem & (n_mem - 1):
            return lax.rem(me + n_mem - d, n_mem)
        return flipped(d)

    def flipped(d):
        p = me
        bit = 1
        while bit < n_mem:
            if d & bit:
                p = p + bit - 2 * bit * lax.rem(lax.div(me, bit), 2)
            bit *= 2
        return p

    def cols(p):
        return pl.ds(pl.multiple_of(p * variables, variables), variables)

    def block_rows(p):
        return rows_at(p * block, block)

    def sample_rows(p):
        return rows_at(p * samples, samples)

    loads = [
        pltpu.make_async_copy(prior.at[:, cols(me)], x.at[block_rows(me), cols(sp)], local.at[0]),
        pltpu.make_async_copy(terminal.at[sample_rows(sp), :], z.at[:, cols(sp)], local.at[1]),
        pltpu.make_async_copy(angles, seen.at[:, cols(sp)], local.at[2]),
        pltpu.make_async_copy(
            perturbation.at[:, sample_rows(sp), :], noise.at[:, :, cols(sp)], local.at[3]
        ),
    ]
    for copy in loads:
        copy.start()

    barrier = pltpu.get_barrier_semaphore()
    greet = [(space_at(d), me) for d in range(1, n_space)]
    greet += [(sp, mem_to(d)) for d in range(1, n_mem)]
    for dev in greet:
        pl.semaphore_signal(barrier, inc=1, device_id=dev, device_id_type=MESH)
    pl.semaphore_wait(barrier, len(greet))

    sent = []

    def remote(src, dst, out_sem, in_sem, dev):
        copy = pltpu.make_async_remote_copy(
            src_ref=src,
            dst_ref=dst,
            send_sem=out_sem,
            recv_sem=in_sem,
            device_id=dev,
            device_id_type=MESH,
        )
        copy.start()
        sent.append(copy)
        return copy

    used = [0]

    def put_once(src, dst, dev):
        i = used[0]
        used[0] += 1
        return remote(src, dst, once_send.at[i], once_recv.at[i], dev)

    here = x.at[block_rows(me), cols(sp)]
    exchange = [
        put_once(prior.at[:, cols(mem_to(d))], here, (sp, mem_to(d))) for d in range(1, n_mem)
    ]
    firsts = []
    for d in range(1, n_space):
        q = space_at(d)
        firsts.append(put_once(terminal.at[sample_rows(q), :], z.at[:, cols(sp)], (q, me)))
        firsts.append(put_once(angles, seen.at[:, cols(sp)], (q, me)))

    over_x, to_core = [], []

    def pass_on(src, at):
        over_x.append([put_once(src, at, (x_at(d), me)) for d in range(1, nx)])
        to_core.append(put_once(src, at, partner))

    pass_on(prior.at[:, cols(me)], here)
    for d, copy in enumerate(exchange, 1):
        copy.wait_recv()
        at = x.at[block_rows(mem_from(d)), cols(sp)]
        pass_on(at, at)
    onward = []
    for b, group in enumerate(over_x):
        origin = mem_from(b) if b else me
        for d, copy in enumerate(group, 1):
            copy.wait_recv()
            at = x.at[block_rows(origin), cols(x_at(-d))]
            onward.append(put_once(at, at, partner))
    for copy in loads[:3]:
        copy.wait()
    norms = jnp.zeros((SUBLANES, members), jnp.float32)

    def take(where):
        xs = x[:, where]
        for j, piece in enumerate(split(xs, PARTS)):
            xb[j, :, where] = piece
        total = jnp.zeros((SUBLANES, members), jnp.float32)
        for piece in reversed(split(xs * xs, 3)):
            total = total + lax.dot_general(
                jnp.ones((SUBLANES, xs.shape[1]), jnp.bfloat16),
                piece,
                (((1,), (1,)), ((), ())),
                preferred_element_type=jnp.float32,
            )
        return total

    for d in range(nx):
        norms = norms + take(cols(x_at(d)))
    for copy in to_core + onward + firsts:
        copy.wait_recv()
    for d in range(nx):
        norms = norms + take(cols(lax.rem(xi + d, nx) * CORES + 1 - core))
    norms = norms[:1]
    parts = [xb[j] for j in range(PARTS)]

    inbound = {}

    def chunk_rows(c):
        return pl.ds(c * rows, rows)

    def owned():
        return rows_at(me * own_rows, own_rows) if scatter else pl.ds(0, rows)

    def send_noise(k):
        return [
            put_once(
                perturbation.at[k, sample_rows(space_at(d)), :],
                noise.at[k, :, cols(sp)],
                (space_at(d), me),
            )
            for d in range(1, n_space)
        ]

    def send_sums(k, c):
        alpha = constants(k)[1]
        gram[k, c] = 2.0 * alpha * product(z[chunk_rows(c), :], parts, 1) - alpha * alpha * norms
        inbound["sums", k, c] = []
        for d in range(1, n_mem):
            p = mem_to(d)
            src = gram.at[k, c, rows_at(p * own_rows, own_rows), :] if scatter else gram.at[k, c]
            inbound["sums", k, c].append(
                remote(
                    src,
                    sums.at[k, c, d - 1],
                    sum_send.at[k, c, d - 1],
                    sum_recv.at[k, c, d - 1],
                    (sp, p),
                )
            )

    def send_weights(k, c):
        total = gram[k, c, owned(), :]
        for d, copy in enumerate(inbound["sums", k, c]):
            copy.wait_recv()
            total = total + sums[k, c, d]
        logits = total / (2.0 * constants(k)[0] * temper)
        e = jnp.exp(logits - jnp.max(logits, axis=1, keepdims=True))
        w[k, c, owned(), :] = e / jnp.sum(e, axis=1, keepdims=True)
        inbound["give", k, c] = []
        if scatter:
            at = w.at[k, c, owned(), :]
            inbound["give", k, c] = [
                remote(
                    at, at, give_send.at[k, c, d - 1], give_recv.at[k, c, d - 1], (sp, mem_to(d))
                )
                for d in range(1, n_mem)
            ]

    def advance(k, c):
        t, alpha, drift, g2, damp = constants(k)
        zs = z[chunk_rows(c), :]
        seen_term = damp * 4.0 * (seen[...] - arctan(zs)) / (1.0 + zs * zs)
        z[chunk_rows(c), :] = (
            zs
            + dt * (-drift * zs + g2 * (seen_term - zs / t))
            + math.sqrt(dt * g2) * noise[k, chunk_rows(c), :]
        )

    def add_blend(k, c):
        t, alpha, _, g2, _ = constants(k)
        for copy in inbound["give", k, c]:
            copy.wait_recv()
        blend = product(w[k, c], parts, 0)
        z[chunk_rows(c), :] = z[chunk_rows(c), :] + (dt * g2 * alpha / t) * blend

    each = list(range(chunks))
    results = []
    arriving = {}
    for k in range(ITERS):
        for c in each:
            if k > 0:
                add_blend(k - 1, c)
            send_sums(k, c)
        if k == 0:
            arriving[0] = send_noise(0)
        for c in each:
            send_weights(k, c)
        if k + 1 < ITERS:
            arriving[k + 1] = send_noise(k + 1)
        if k == 0:
            loads[3].wait()
        for copy in arriving[k]:
            copy.wait_recv()
        for c in each:
            advance(k, c)
    for c in each:
        add_blend(ITERS - 1, c)
        target = out.at[rows_at(sp * samples + c * rows, rows), :]
        results += [
            put_once(z.at[chunk_rows(c), cols(space_at(d))], target, (space_at(d), me))
            for d in range(1, n_space)
        ]
        own = pltpu.make_async_copy(z.at[chunk_rows(c), cols(sp)], target, local.at[4 + c])
        own.start()
        loads.append(own)
    for copy in loads[4:]:
        copy.wait()
    for copy in results:
        copy.wait_recv()
    for copy in sent:
        copy.wait_send()


def per_device(prior, terminal, perturbation, angles):
    n_space, n_mem = lax.axis_size("space"), lax.axis_size("mem")
    all_samples, variables = terminal.shape
    members = prior.shape[0] * n_mem
    samples = all_samples // n_space
    chunks = CHUNKS
    while chunks > 1 and samples % (chunks * n_mem * SUBLANES):
        chunks //= 2
    rows = samples // chunks
    scatter = rows % (n_mem * SUBLANES) == 0
    own_rows = rows // n_mem if scatter else rows
    wide = n_space * variables
    temper = math.sqrt(wide * n_mem)
    f32 = jnp.float32
    nx = n_space // CORES
    iters = perturbation.shape[0]
    once = n_mem - 1 + (2 + iters + chunks) * (n_space - 1) + n_mem * (2 * nx - 1)
    operands = prior, terminal, perturbation, angles.reshape(1, variables)
    anywhere = pl.BlockSpec(memory_space=pl.ANY)
    return pl.pallas_call(
        functools.partial(kernel, (n_space, n_mem, scatter, temper)),
        out_shape=jax.ShapeDtypeStruct((all_samples, variables), f32),
        in_specs=[anywhere] * 4,
        out_specs=anywhere,
        scratch_shapes=[
            pltpu.VMEM((members, wide), f32),
            pltpu.VMEM((samples, wide), f32),
            pltpu.VMEM((iters, samples, wide), f32),
            pltpu.VMEM((1, wide), f32),
            pltpu.VMEM((iters, chunks, rows, members), f32),
            pltpu.VMEM((iters, chunks, n_mem - 1, own_rows, members), f32),
            pltpu.VMEM((iters, chunks, rows, members), f32),
            pltpu.VMEM((PARTS, members, wide), jnp.bfloat16),
            pltpu.SemaphoreType.DMA((iters, chunks, n_mem - 1)),
            pltpu.SemaphoreType.DMA((iters, chunks, n_mem - 1)),
            pltpu.SemaphoreType.DMA((iters, chunks, n_mem - 1)),
            pltpu.SemaphoreType.DMA((iters, chunks, n_mem - 1)),
            pltpu.SemaphoreType.DMA((once,)),
            pltpu.SemaphoreType.DMA((once,)),
            pltpu.SemaphoreType.DMA((4 + chunks,)),
        ],
        compiler_params=pltpu.CompilerParams(
            collective_id=0, has_side_effects=True, vmem_limit_bytes=VMEM_LIMIT
        ),
    )(*[pltpu.with_memory_space_constraint(a, pltpu.HBM) for a in operands])


def solution(mesh):
    in_specs = (
        P("mem", "space"),
        P(None, ("space", "mem")),
        P(None, None, ("space", "mem")),
        P(("space", "mem")),
    )
    out_specs = P(None, ("space", "mem"))
    return jax.shard_map(
        per_device, mesh=mesh, in_specs=in_specs, out_specs=out_specs, check_vma=False
    )
```

time: 77.3 us -> 73.6 us (0.952)
  Pallas kernels: 75.3 us -> 72.7 us
  local copies, waits for them, and re-layouts: 1.87 us -> 0.8 us
    pallas_call x1, Pallas kernels: 75.3 us -> 72.7 us  [per_device(): pl.pallas_call(functools.partial(kernel, (n_space, n_mem, scatter, temper...]
    unnamed x1, local copies, waits for them, and re-layouts: 1.87 us -> 0.8 us
where the time goes in v2:
time: 73.6 us; the launch traced here: 73.5 us
  Pallas kernels  72.7 us (99%)
  local copies, waits for them, and re-layouts  0.8 us (1%)
    pallas_call x1, Pallas kernels, per_device(): pl.pallas_call(functools.partial(kernel, (n_space, n_mem, scatter, temper...  72.7 us

profile of v2, /device:TPU:0, one launch (start us, length us, event | category | flops | bytes accessed | tf_op | source)
XLA Modules:
  0.0 73.5 jit_solution(1788457895591337189)
XLA Ops:
  0.0 72.7 %shard_map.46 = f32[512,256]{1,0:T(8,128)S(1)} custom-call(f32[64,2048]{1,0:T(8,128)} %prior.1, f32[512,256]{1,0:T(8,128)} %terminal.1, f32[3,512,256]{2,1,0:T(8,128)} %perturbation.1, f32[1,256]{1,0:T(1,128)} %bitcast.1), custom_call_target="tpu_custom_call" | custom-call | tf_op jit(solution)/shard_map/pallas_call | solution.py:366
  72.7 0.8 %copy.6 = f32[512,256]{1,0:T(8,128)} copy(f32[512,256]{1,0:T(8,128)S(1)} %shard_map.46) | data formatting | bytes 1048576

commit v3 on v2

v3 whole, which is shorter than its diff:
```python
import functools
import math

import jax
import jax.numpy as jnp
from jax import lax
from jax.experimental import pallas as pl
from jax.experimental.pallas import tpu as pltpu
from jax.sharding import PartitionSpec as P

ITERS = 3
CHUNKS = 2
PARTS = 2
VMEM_LIMIT = 48 << 20
CORES = 2
SUBLANES = 8
LANES = 128
MESH = pl.DeviceIdType.MESH


def split(a, parts):
    out = []
    for _ in range(parts):
        out.append(a.astype(jnp.bfloat16))
        a = a - out[-1].astype(jnp.float32)
    return out


def product(a, parts, contract_b):
    n = a.shape[0]
    lhs = split(a, len(parts))
    total = None
    for i in reversed(range(len(parts))):
        rows = lhs[: len(parts) - i]
        both = lax.dot_general(
            jnp.concatenate(rows, axis=0),
            parts[i],
            (((1,), (contract_b,)), ((), ())),
            preferred_element_type=jnp.float32,
        )
        for j in reversed(range(len(rows))):
            term = both[j * n : (j + 1) * n]
            total = term if total is None else total + term
    return total


def arctan(x):
    a = jnp.abs(x)
    big = a > 2.414213562373095
    mid = a > 0.4142135623730950
    num = jnp.where(big, -1.0, jnp.where(mid, a - 1.0, a))
    den = jnp.where(big, a, jnp.where(mid, a + 1.0, 1.0))
    base = jnp.where(big, math.pi / 2, jnp.where(mid, math.pi / 4, 0.0))
    r = num / den
    s = r * r
    poly = ((8.05374449538e-2 * s - 1.38776856032e-1) * s + 1.99777106478e-1) * s
    poly = (poly - 3.33329491539e-1) * s * r + r
    y = base + poly
    return jnp.where(x < 0.0, -y, y)


def rows_at(start, size):
    return pl.ds(pl.multiple_of(start, SUBLANES), size)


def constants(k):
    t = 1.0 - k / ITERS
    alpha = 1.0 - 0.5 * t
    return t, alpha, -0.5 / alpha, 1.0 + t / alpha, 1.0 - t


def kernel(
    plan,
    prior,
    terminal,
    perturbation,
    angles,
    out,
    x,
    z,
    noise,
    seen,
    gram,
    sums,
    w,
    xb,
    xt,
    norms,
    send,
    recv,
    local,
):
    n_space, n_mem, scatter, temper = plan
    _, chunks, rows, members = gram.shape
    own_rows = rows // n_mem if scatter else rows
    samples = z.shape[0]
    block = prior.shape[0]
    variables = terminal.shape[1]
    nx = n_space // CORES
    dt = 1.0 / ITERS

    sp = lax.axis_index("space")
    me = lax.axis_index("mem")
    core = lax.rem(sp, CORES)
    xi = lax.div(sp, CORES)
    partner = (xi * CORES + 1 - core, me)

    def space_at(d):
        return lax.rem(sp + d + n_space, n_space)

    def x_at(d):
        return lax.rem(xi + d + nx, nx) * CORES + core

    def pair(d):
        p = me
        bit = 1
        while bit < n_mem:
            if d & bit:
                p = p + bit - 2 * bit * lax.rem(lax.div(me, bit), 2)
            bit *= 2
        return p

    def cols(p):
        return pl.ds(pl.multiple_of(p * variables, variables), variables)

    def block_rows(p):
        return rows_at(p * block, block)

    def chunk_rows(c):
        return pl.ds(c * rows, rows)

    def sample_rows(p):
        return rows_at(p * samples, samples)

    loads = [
        pltpu.make_async_copy(prior.at[:, cols(me)], x.at[sp, block_rows(me), :], local.at[0]),
        pltpu.make_async_copy(terminal.at[sample_rows(sp), :], z.at[:, cols(sp)], local.at[1]),
        pltpu.make_async_copy(angles, seen.at[:, cols(sp)], local.at[2]),
        pltpu.make_async_copy(
            perturbation.at[:, sample_rows(sp), :], noise.at[:, :, cols(sp)], local.at[3]
        ),
    ]
    for copy in loads:
        copy.start()

    barrier = pltpu.get_barrier_semaphore()
    greet = [(space_at(d), me) for d in range(1, n_space)]
    greet += [(sp, pair(d)) for d in range(1, n_mem)]
    for dev in greet:
        pl.semaphore_signal(barrier, inc=1, device_id=dev, device_id_type=MESH)
    pl.semaphore_wait(barrier, len(greet))

    together = max(1, LANES // block)
    groups = range(n_mem // together)
    slots = {}
    pending = {}

    def put(key, src, dst, dev):
        i = slots.setdefault(key, len(slots))
        if i in pending:
            pending[i].wait_send()
        pending[i] = pltpu.make_async_remote_copy(
            src_ref=src,
            dst_ref=dst,
            send_sem=send.at[i],
            recv_sem=recv.at[i],
            device_id=dev,
            device_id_type=MESH,
        )
        pending[i].start()
        return pending[i]

    here = x.at[sp, block_rows(me), :]
    exchange = {
        d: put(("mem", d), prior.at[:, cols(pair(d))], here, (sp, pair(d)))
        for d in range(1, n_mem)
    }

    def send_start(c):
        copies = []
        for d in range(1, n_space):
            q = space_at(d)
            src = terminal.at[rows_at(q * samples + c * rows, rows), :]
            copies.append(put(("space", c, d), src, z.at[chunk_rows(c), cols(sp)], (q, me)))
        return copies

    starts = [send_start(0)]

    over_x, to_core, onward = [], [], []

    def group_at(i):
        return rows_at(lax.div(pair(i * together), together) * together * block, together * block)

    def group_blocks(i):
        return range(i * together, (i + 1) * together)

    def pass_on(b, src, at):
        over_x.append(
            [put(("x", b, d), src, at, (x_at(d), me)) for d in range(1, nx)]
        )

    def pass_core(i):
        for b in group_blocks(i):
            for copy in over_x[b]:
                copy.wait_recv()
        onward.append([])
        for d in range(1, nx):
            at = x.at[x_at(-d), group_at(i), :]
            onward[i].append(put(("onward", i, d), at, at, partner))

    def take(q, i):
        some = group_at(i)
        xs = x[q, some, :]
        for j, piece in enumerate(split(xs, PARTS)):
            xb[j, some, cols(q)] = piece
        turned = xs.T
        for j, piece in enumerate(split(turned, PARTS)):
            xt[j, cols(q), some] = piece
        norms[:, some] = norms[:, some] + jnp.sum(turned * turned, axis=0, keepdims=True)

    norms[...] = jnp.zeros_like(norms)
    pass_on(0, prior.at[:, cols(me)], here)
    loads[0].wait()
    for i in groups:
        for d in group_blocks(i):
            if d:
                exchange[d].wait_recv()
                at = x.at[sp, block_rows(pair(d)), :]
                pass_on(d, at, at)
        at = x.at[sp, group_at(i), :]
        to_core.append(put(("core", i), at, at, partner))
        take(sp, i)
    starts += [send_start(c) for c in range(1, chunks)]
    firsts = [
        put(("angles", d), angles, seen.at[:, cols(sp)], (space_at(d), me))
        for d in range(1, n_space)
    ]
    for copy in loads[1:3]:
        copy.wait()

    inbound = {}

    def owned():
        return rows_at(me * own_rows, own_rows) if scatter else pl.ds(0, rows)

    def send_noise(k):
        return [
            put(
                ("noise", k, d),
                perturbation.at[k, sample_rows(space_at(d)), :],
                noise.at[k, :, cols(sp)],
                (space_at(d), me),
            )
            for d in range(1, n_space)
        ]

    def send_sums(k, c, i=None):
        alpha = constants(k)[1]
        some = pl.ds(0, members) if i is None else group_at(i)
        parts = [xt[j, :, some] for j in range(PARTS)]
        inner = product(z[chunk_rows(c), :], parts, 0)
        gram[k, c, :, some] = 2.0 * alpha * inner - alpha * alpha * norms[:, some]
        for d in range(1, n_mem):
            rows_to = rows_at(pair(d) * own_rows, own_rows) if scatter else pl.ds(0, rows)
            inbound["sums", k, c].append(
                put(
                    ("sums", c, i or 0, d),
                    gram.at[k, c, rows_to, some],
                    sums.at[k, c, d - 1, :, some],
                    (sp, pair(d)),
                )
            )

    def send_weights(k, c):
        total = gram[k, c, owned(), :]
        for copy in inbound["sums", k, c]:
            copy.wait_recv()
        for d in range(n_mem - 1):
            total = total + sums[k, c, d]
        logits = total / (2.0 * constants(k)[0] * temper)
        e = jnp.exp(logits - jnp.max(logits, axis=1, keepdims=True))
        w[k, c, owned(), :] = e / jnp.sum(e, axis=1, keepdims=True)
        inbound["give", k, c] = []
        if scatter:
            at = w.at[k, c, owned(), :]
            inbound["give", k, c] = [
                put(("give", c, d) if c else ("mem", d), at, at, (sp, pair(d)))
                for d in range(1, n_mem)
            ]

    def advance(k, c):
        t, alpha, drift, g2, damp = constants(k)
        zs = z[chunk_rows(c), :]
        seen_term = damp * 4.0 * (seen[...] - arctan(zs)) / (1.0 + zs * zs)
        z[chunk_rows(c), :] = (
            zs
            + dt * (-drift * zs + g2 * (seen_term - zs / t))
            + math.sqrt(dt * g2) * noise[k, chunk_rows(c), :]
        )

    def add_blend(k, c):
        t, alpha, _, g2, _ = constants(k)
        for copy in inbound["give", k, c]:
            copy.wait_recv()
        blend = product(w[k, c], [xb[j] for j in range(PARTS)], 0)
        z[chunk_rows(c), :] = z[chunk_rows(c), :] + (dt * g2 * alpha / t) * blend

    each = list(range(chunks))
    results = []
    arriving = {}
    for k in range(ITERS):
        for c in each:
            inbound["sums", k, c] = []
    for copy in starts[0]:
        copy.wait_recv()

    def finish_group(i):
        for copy in onward[i]:
            copy.wait_recv()
        for d in range(1, nx):
            take(lax.rem(xi + d, nx) * CORES + 1 - core, i)
        send_sums(0, 0, i)

    for i in groups:
        pass_core(i)
        for d in range(1, nx):
            take(x_at(d), i)
        to_core[i].wait_recv()
        take(xi * CORES + 1 - core, i)
        if i:
            finish_group(i - 1)
    finish_group(len(groups) - 1)
    for k in range(ITERS):
        for c in each:
            if k > 0:
                add_blend(k - 1, c)
            elif c > 0:
                for copy in starts[c]:
                    copy.wait_recv()
            if k + c > 0:
                send_sums(k, c)
        if k == 0:
            arriving[0] = send_noise(0)
        for c in each:
            send_weights(k, c)
        if k + 1 < ITERS:
            arriving[k + 1] = send_noise(k + 1)
        if k == 0:
            loads[3].wait()
            for copy in firsts:
                copy.wait_recv()
        for copy in arriving[k]:
            copy.wait_recv()
        for c in each:
            advance(k, c)
    for c in each:
        add_blend(ITERS - 1, c)
        target = out.at[rows_at(sp * samples + c * rows, rows), :]
        results += [
            put(("space", c, d), z.at[chunk_rows(c), cols(space_at(d))], target, (space_at(d), me))
            for d in range(1, n_space)
        ]
        own = pltpu.make_async_copy(z.at[chunk_rows(c), cols(sp)], target, local.at[4 + c])
        own.start()
        loads.append(own)
    for copy in loads[4:]:
        copy.wait()
    for copy in results:
        copy.wait_recv()
    for copy in pending.values():
        copy.wait_send()


def per_device(prior, terminal, perturbation, angles):
    n_space, n_mem = lax.axis_size("space"), lax.axis_size("mem")
    all_samples, variables = terminal.shape
    members = prior.shape[0] * n_mem
    samples = all_samples // n_space
    chunks = CHUNKS
    while chunks > 1 and samples % (chunks * n_mem * SUBLANES):
        chunks //= 2
    rows = samples // chunks
    scatter = rows % (n_mem * SUBLANES) == 0
    own_rows = rows // n_mem if scatter else rows
    block = prior.shape[0]
    groups = n_mem // max(1, LANES // block)
    wide = n_space * variables
    assert n_mem & (n_mem - 1) == 0
    temper = math.sqrt(wide * n_mem)
    f32 = jnp.float32
    nx = n_space // CORES
    iters = perturbation.shape[0]
    steps = (groups + 2 * chunks - 1) * (n_mem - 1)
    slots = steps + (chunks + 1 + iters) * (n_space - 1) + n_mem * (nx - 1) + groups * nx
    operands = prior, terminal, perturbation, angles.reshape(1, variables)
    anywhere = pl.BlockSpec(memory_space=pl.ANY)
    return pl.pallas_call(
        functools.partial(kernel, (n_space, n_mem, scatter, temper)),
        out_shape=jax.ShapeDtypeStruct((all_samples, variables), f32),
        in_specs=[anywhere] * 4,
        out_specs=anywhere,
        scratch_shapes=[
            pltpu.VMEM((n_space, members, variables), f32),
            pltpu.VMEM((samples, wide), f32),
            pltpu.VMEM((iters, samples, wide), f32),
            pltpu.VMEM((1, wide), f32),
            pltpu.VMEM((iters, chunks, rows, members), f32),
            pltpu.VMEM((iters, chunks, n_mem - 1, own_rows, members), f32),
            pltpu.VMEM((iters, chunks, rows, members), f32),
            pltpu.VMEM((PARTS, members, wide), jnp.bfloat16),
            pltpu.VMEM((PARTS, wide, members), jnp.bfloat16),
            pltpu.VMEM((1, members), f32),
            pltpu.SemaphoreType.DMA((slots,)),
            pltpu.SemaphoreType.DMA((slots,)),
            pltpu.SemaphoreType.DMA((4 + chunks,)),
        ],
        compiler_params=pltpu.CompilerParams(
            collective_id=0, has_side_effects=True, vmem_limit_bytes=VMEM_LIMIT
        ),
    )(*[pltpu.with_memory_space_constraint(a, pltpu.HBM) for a in operands])


def solution(mesh):
    in_specs = (
        P("mem", "space"),
        P(None, ("space", "mem")),
        P(None, None, ("space", "mem")),
        P(("space", "mem")),
    )
    out_specs = P(None, ("space", "mem"))
    return jax.shard_map(
        per_device, mesh=mesh, in_specs=in_specs, out_specs=out_specs, check_vma=False
    )
```

time: 73.6 us -> 68.3 us (0.928)
  Pallas kernels: 72.7 us -> 67.4 us
    pallas_call x1, Pallas kernels: 72.7 us -> 67.4 us  [per_device(): pl.pallas_call(functools.partial(kernel, (n_space, n_mem, scatter, temper...]
where the time goes in v3:
time: 68.3 us; the launch traced here: 68.2 us
  Pallas kernels  67.4 us (99%)
  local copies, waits for them, and re-layouts  0.8 us (1%)
    pallas_call x1, Pallas kernels, per_device(): pl.pallas_call(functools.partial(kernel, (n_space, n_mem, scatter, temper...  67.4 us

profile of v3, /device:TPU:0, one launch (start us, length us, event | category | flops | bytes accessed | tf_op | source)
XLA Modules:
  0.0 68.2 jit_solution(1291385814549734193)
XLA Ops:
  0.0 67.4 %shard_map.46 = f32[512,256]{1,0:T(8,128)S(1)} custom-call(f32[64,2048]{1,0:T(8,128)} %prior.1, f32[512,256]{1,0:T(8,128)} %terminal.1, f32[3,512,256]{2,1,0:T(8,128)} %perturbation.1, f32[1,256]{1,0:T(1,128)} %bitcast.1), custom_call_target="tpu_custom_call" | custom-call | tf_op jit(solution)/shard_map/pallas_call | solution.py:397
  67.4 0.8 %copy.6 = f32[512,256]{1,0:T(8,128)} copy(f32[512,256]{1,0:T(8,128)S(1)} %shard_map.46) | data formatting | bytes 1048576

commit v4 on v3

--- a/solution.py
+++ b/solution.py
@@ -10,6 +10,7 @@
 
 ITERS = 3
 CHUNKS = 2
+PIECE = 8
 PARTS = 2
 VMEM_LIMIT = 48 << 20
 CORES = 2
@@ -91,8 +92,8 @@
     local,
 ):
     n_space, n_mem, scatter, temper = plan
-    _, chunks, rows, members = gram.shape
-    own_rows = rows // n_mem if scatter else rows
+    _, chunks, pieces, own_rows, members = gram.shape
+    rows = pieces * own_rows
     samples = z.shape[0]
     block = prior.shape[0]
     variables = terminal.shape[1]
@@ -155,11 +156,9 @@
     slots = {}
     pending = {}
 
-    def put(key, src, dst, dev):
+    def copy_at(key, src, dst, dev):
         i = slots.setdefault(key, len(slots))
-        if i in pending:
-            pending[i].wait_send()
-        pending[i] = pltpu.make_async_remote_copy(
+        return pltpu.make_async_remote_copy(
             src_ref=src,
             dst_ref=dst,
             send_sem=send.at[i],
@@ -167,10 +166,20 @@
             device_id=dev,
             device_id_type=MESH,
         )
-        pending[i].start()
-        return pending[i]
+
+    def put(key, src, dst, dev):
+        return put_all(key, [(src, dst, dev)], dst)
+
+    def put_all(key, copies, landing):
+        if key in pending:
+            pending[key].wait_send()
+        for src, dst, dev in copies:
+            copy_at(key, src, dst, dev).start()
+        pending[key] = copy_at(key, landing, landing, copies[0][2])
+        return pending[key]
 
     here = x.at[sp, block_rows(me), :]
+    others = pl.ds(0, (n_space - 1) * variables)
     exchange = {
         d: put(("mem", d), prior.at[:, cols(pair(d))], here, (sp, pair(d)))
         for d in range(1, n_mem)
@@ -181,8 +190,8 @@
         for d in range(1, n_space):
             q = space_at(d)
             src = terminal.at[rows_at(q * samples + c * rows, rows), :]
-            copies.append(put(("space", c, d), src, z.at[chunk_rows(c), cols(sp)], (q, me)))
-        return copies
+            copies.append((src, z.at[chunk_rows(c), cols(sp)], (q, me)))
+        return put_all(("space", c), copies, z.at[chunk_rows(c), others])
 
     starts = [send_start(0)]
 
@@ -231,62 +240,54 @@
         to_core.append(put(("core", i), at, at, partner))
         take(sp, i)
     starts += [send_start(c) for c in range(1, chunks)]
-    firsts = [
-        put(("angles", d), angles, seen.at[:, cols(sp)], (space_at(d), me))
-        for d in range(1, n_space)
-    ]
+    firsts = put_all(
+        "angles",
+        [(angles, seen.at[:, cols(sp)], (space_at(d), me)) for d in range(1, n_space)],
+        seen.at[:, others],
+    )
     for copy in loads[1:3]:
         copy.wait()
 
     inbound = {}
 
-    def owned():
-        return rows_at(me * own_rows, own_rows) if scatter else pl.ds(0, rows)
+    owned = me if scatter else 0
 
     def send_noise(k):
-        return [
-            put(
-                ("noise", k, d),
-                perturbation.at[k, sample_rows(space_at(d)), :],
-                noise.at[k, :, cols(sp)],
-                (space_at(d), me),
-            )
-            for d in range(1, n_space)
-        ]
+        copies = []
+        for d in range(1, n_space):
+            q = space_at(d)
+            src = perturbation.at[k, sample_rows(q), :]
+            copies.append((src, noise.at[k, :, cols(sp)], (q, me)))
+        return put_all(("noise", k), copies, noise.at[k, :, others])
 
     def send_sums(k, c, i=None):
         alpha = constants(k)[1]
         some = pl.ds(0, members) if i is None else group_at(i)
         parts = [xt[j, :, some] for j in range(PARTS)]
         inner = product(z[chunk_rows(c), :], parts, 0)
-        gram[k, c, :, some] = 2.0 * alpha * inner - alpha * alpha * norms[:, some]
+        value = 2.0 * alpha * inner - alpha * alpha * norms[:, some]
+        gram[k, c, :, :, some] = value.reshape(pieces, own_rows, value.shape[1])
+        copies = []
         for d in range(1, n_mem):
-            rows_to = rows_at(pair(d) * own_rows, own_rows) if scatter else pl.ds(0, rows)
-            inbound["sums", k, c].append(
-                put(
-                    ("sums", c, i or 0, d),
-                    gram.at[k, c, rows_to, some],
-                    sums.at[k, c, d - 1, :, some],
-                    (sp, pair(d)),
-                )
-            )
+            src = gram.at[k, c, pair(d) if scatter else 0, :, some]
+            copies.append((src, sums.at[k, c, d - 1, :, some], (sp, pair(d))))
+        landing = sums.at[k, c, :, :, some]
+        inbound["sums", k, c].append(put_all(("sums", c, i or 0), copies, landing))
 
     def send_weights(k, c):
-        total = gram[k, c, owned(), :]
+        total = gram[k, c, owned]
         for copy in inbound["sums", k, c]:
             copy.wait_recv()
         for d in range(n_mem - 1):
             total = total + sums[k, c, d]
         logits = total / (2.0 * constants(k)[0] * temper)
         e = jnp.exp(logits - jnp.max(logits, axis=1, keepdims=True))
-        w[k, c, owned(), :] = e / jnp.sum(e, axis=1, keepdims=True)
-        inbound["give", k, c] = []
+        w[k, c, owned] = e / jnp.sum(e, axis=1, keepdims=True)
         if scatter:
-            at = w.at[k, c, owned(), :]
-            inbound["give", k, c] = [
-                put(("give", c, d) if c else ("mem", d), at, at, (sp, pair(d)))
-                for d in range(1, n_mem)
-            ]
+            at = w.at[k, c, owned]
+            copies = [(at, at, (sp, pair(d))) for d in range(1, n_mem)]
+            landing = w.at[k, c, pl.ds(0, n_mem - 1)]
+            inbound["give", k, c] = put_all(("give", c), copies, landing)
 
     def advance(k, c):
         t, alpha, drift, g2, damp = constants(k)
@@ -300,9 +301,9 @@
 
     def add_blend(k, c):
         t, alpha, _, g2, _ = constants(k)
-        for copy in inbound["give", k, c]:
-            copy.wait_recv()
-        blend = product(w[k, c], [xb[j] for j in range(PARTS)], 0)
+        if scatter:
+            inbound["give", k, c].wait_recv()
+        blend = product(w[k, c].reshape(rows, members), [xb[j] for j in range(PARTS)], 0)
         z[chunk_rows(c), :] = z[chunk_rows(c), :] + (dt * g2 * alpha / t) * blend
 
     each = list(range(chunks))
@@ -311,8 +312,7 @@
     for k in range(ITERS):
         for c in each:
             inbound["sums", k, c] = []
-    for copy in starts[0]:
-        copy.wait_recv()
+    starts[0].wait_recv()
 
     def finish_group(i):
         for copy in onward[i]:
@@ -335,8 +335,7 @@
             if k > 0:
                 add_blend(k - 1, c)
             elif c > 0:
-                for copy in starts[c]:
-                    copy.wait_recv()
+                starts[c].wait_recv()
             if k + c > 0:
                 send_sums(k, c)
         if k == 0:
@@ -347,19 +346,18 @@
             arriving[k + 1] = send_noise(k + 1)
         if k == 0:
             loads[3].wait()
-            for copy in firsts:
-                copy.wait_recv()
-        for copy in arriving[k]:
-            copy.wait_recv()
+            firsts.wait_recv()
+        arriving[k].wait_recv()
         for c in each:
             advance(k, c)
     for c in each:
         add_blend(ITERS - 1, c)
         target = out.at[rows_at(sp * samples + c * rows, rows), :]
-        results += [
-            put(("space", c, d), z.at[chunk_rows(c), cols(space_at(d))], target, (space_at(d), me))
-            for d in range(1, n_space)
-        ]
+        copies = []
+        for d in range(1, n_space):
+            q = space_at(d)
+            copies.append((z.at[chunk_rows(c), cols(q)], target, (q, me)))
+        results.append(put_all(("space", c), copies, z.at[chunk_rows(c), others]))
         own = pltpu.make_async_copy(z.at[chunk_rows(c), cols(sp)], target, local.at[4 + c])
         own.start()
         loads.append(own)
@@ -377,11 +375,12 @@
     members = prior.shape[0] * n_mem
     samples = all_samples // n_space
     chunks = CHUNKS
-    while chunks > 1 and samples % (chunks * n_mem * SUBLANES):
+    while chunks > 1 and samples % (chunks * n_mem * PIECE):
         chunks //= 2
     rows = samples // chunks
-    scatter = rows % (n_mem * SUBLANES) == 0
-    own_rows = rows // n_mem if scatter else rows
+    scatter = rows % (n_mem * PIECE) == 0
+    pieces = n_mem if scatter else 1
+    own_rows = rows // pieces
     block = prior.shape[0]
     groups = n_mem // max(1, LANES // block)
     wide = n_space * variables
@@ -390,8 +389,7 @@
     f32 = jnp.float32
     nx = n_space // CORES
     iters = perturbation.shape[0]
-    steps = (groups + 2 * chunks - 1) * (n_mem - 1)
-    slots = steps + (chunks + 1 + iters) * (n_space - 1) + n_mem * (nx - 1) + groups * nx
+    slots = n_mem - 1 + n_mem * (nx - 1) + groups * (nx + 1) + 3 * chunks + iters
     operands = prior, terminal, perturbation, angles.reshape(1, variables)
     anywhere = pl.BlockSpec(memory_space=pl.ANY)
     return pl.pallas_call(
@@ -404,9 +402,9 @@
             pltpu.VMEM((samples, wide), f32),
             pltpu.VMEM((iters, samples, wide), f32),
             pltpu.VMEM((1, wide), f32),
-            pltpu.VMEM((iters, chunks, rows, members), f32),
+            pltpu.VMEM((iters, chunks, pieces, own_rows, members), f32),
             pltpu.VMEM((iters, chunks, n_mem - 1, own_rows, members), f32),
-            pltpu.VMEM((iters, chunks, rows, members), f32),
+            pltpu.VMEM((iters, chunks, pieces, own_rows, members), f32),
             pltpu.VMEM((PARTS, members, wide), jnp.bfloat16),
             pltpu.VMEM((PARTS, wide, members), jnp.bfloat16),
             pltpu.VMEM((1, members), f32),

time: 68.3 us -> 66.8 us (0.978)
  Pallas kernels: 67.4 us -> 65.8 us
    pallas_call x1, Pallas kernels: 67.4 us -> 65.8 us  [per_device(): pl.pallas_call(functools.partial(kernel, (n_space, n_mem, scatter, temper...]
where the time goes in v4:
time: 66.8 us; the launch traced here: 66.6 us
  Pallas kernels  65.8 us (99%)
  local copies, waits for them, and re-layouts  0.8 us (1%)
    pallas_call x1, Pallas kernels, per_device(): pl.pallas_call(functools.partial(kernel, (n_space, n_mem, scatter, temper...  65.8 us

profile of v4, /device:TPU:0, one launch (start us, length us, event | category | flops | bytes accessed | tf_op | source)
XLA Modules:
  0.0 66.6 jit_solution(6128144632321988193)
XLA Ops:
  0.0 65.8 %shard_map.46 = f32[512,256]{1,0:T(8,128)S(1)} custom-call(f32[64,2048]{1,0:T(8,128)} %prior.1, f32[512,256]{1,0:T(8,128)} %terminal.1, f32[3,512,256]{2,1,0:T(8,128)} %perturbation.1, f32[1,256]{1,0:T(1,128)} %bitcast.1), custom_call_target="tpu_custom_call" | custom-call | tf_op jit(solution)/shard_map/pallas_call | solution.py:395
  65.8 0.8 %copy.6 = f32[512,256]{1,0:T(8,128)} copy(f32[512,256]{1,0:T(8,128)S(1)} %shard_map.46) | data formatting | bytes 1048576

commit v5 on v4

--- a/solution.py
+++ b/solution.py
@@ -268,7 +268,7 @@
         value = 2.0 * alpha * inner - alpha * alpha * norms[:, some]
         gram[k, c, :, :, some] = value.reshape(pieces, own_rows, value.shape[1])
         copies = []
-        for d in range(1, n_mem):
+        for d in reversed(range(1, n_mem)):
             src = gram.at[k, c, pair(d) if scatter else 0, :, some]
             copies.append((src, sums.at[k, c, d - 1, :, some], (sp, pair(d))))
         landing = sums.at[k, c, :, :, some]
@@ -285,7 +285,7 @@
         w[k, c, owned] = e / jnp.sum(e, axis=1, keepdims=True)
         if scatter:
             at = w.at[k, c, owned]
-            copies = [(at, at, (sp, pair(d))) for d in range(1, n_mem)]
+            copies = [(at, at, (sp, pair(d))) for d in reversed(range(1, n_mem))]
             landing = w.at[k, c, pl.ds(0, n_mem - 1)]
             inbound["give", k, c] = put_all(("give", c), copies, landing)
 

time: 66.8 us -> 65.7 us (0.984)
  Pallas kernels: 65.8 us -> 64.7 us
    pallas_call x1, Pallas kernels: 65.8 us -> 64.7 us  [per_device(): pl.pallas_call(functools.partial(kernel, (n_space, n_mem, scatter, temper...]
where the time goes in v5:
time: 65.7 us; the launch traced here: 65.5 us
  Pallas kernels  64.7 us (98%)
  local copies, waits for them, and re-layouts  0.8 us (1%)
    pallas_call x1, Pallas kernels, per_device(): pl.pallas_call(functools.partial(kernel, (n_space, n_mem, scatter, temper...  64.7 us

profile of v5, /device:TPU:0, one launch (start us, length us, event | category | flops | bytes accessed | tf_op | source)
XLA Modules:
  0.0 65.5 jit_solution(4501009404102649791)
XLA Ops:
  0.0 64.7 %shard_map.46 = f32[512,256]{1,0:T(8,128)S(1)} custom-call(f32[64,2048]{1,0:T(8,128)} %prior.1, f32[512,256]{1,0:T(8,128)} %terminal.1, f32[3,512,256]{2,1,0:T(8,128)} %perturbation.1, f32[1,256]{1,0:T(1,128)} %bitcast.1), custom_call_target="tpu_custom_call" | custom-call | tf_op jit(solution)/shard_map/pallas_call | solution.py:395
  64.7 0.8 %copy.6 = f32[512,256]{1,0:T(8,128)} copy(f32[512,256]{1,0:T(8,128)S(1)} %shard_map.46) | data formatting | bytes 1048576

commit v6 on v5

--- a/solution.py
+++ b/solution.py
@@ -107,7 +107,8 @@
     partner = (xi * CORES + 1 - core, me)
 
     def space_at(d):
-        return lax.rem(sp + d + n_space, n_space)
+        over, flip = divmod(n_space - d, CORES)
+        return lax.rem(xi + over, nx) * CORES + lax.rem(core + flip, CORES)
 
     def x_at(d):
         return lax.rem(xi + d + nx, nx) * CORES + core

time: 65.7 us -> 66.8 us (1.017)
  Pallas kernels: 64.7 us -> 65.9 us
    pallas_call x1, Pallas kernels: 64.7 us -> 65.9 us  [per_device(): pl.pallas_call(functools.partial(kernel, (n_space, n_mem, scatter, temper...]
where the time goes in v6:
time: 66.8 us; the launch traced here: 66.7 us
  Pallas kernels  65.9 us (99%)
  local copies, waits for them, and re-layouts  0.8 us (1%)
    pallas_call x1, Pallas kernels, per_device(): pl.pallas_call(functools.partial(kernel, (n_space, n_mem, scatter, temper...  65.9 us

profile of v6, /device:TPU:0, one launch (start us, length us, event | category | flops | bytes accessed | tf_op | source)
XLA Modules:
  0.0 66.7 jit_solution(5974554805062384668)
XLA Ops:
  0.0 65.9 %shard_map.46 = f32[512,256]{1,0:T(8,128)S(1)} custom-call(f32[64,2048]{1,0:T(8,128)} %prior.1, f32[512,256]{1,0:T(8,128)} %terminal.1, f32[3,512,256]{2,1,0:T(8,128)} %perturbation.1, f32[1,256]{1,0:T(1,128)} %bitcast.1), custom_call_target="tpu_custom_call" | custom-call | tf_op jit(solution)/shard_map/pallas_call | solution.py:396
  65.9 0.8 %copy.6 = f32[512,256]{1,0:T(8,128)} copy(f32[512,256]{1,0:T(8,128)S(1)} %shard_map.46) | data formatting | bytes 1048576
